TPU v7x, 32 devices: a whole 2x2x4 slice. The times are simulated.
32 devices in a mesh: head: 4 (over y, x), row: 8 (over z, core).
Axes of the slice: x: 2, y: 2, z: 4, core: 2. Of those that a mesh axis runs over, the one named last changes fastest.
Arguments:
- tokens: bfloat16 [48, 512, 1024], P('row', 'head'), may hold values from -6 to 6
- prev_logits: bfloat16 [48, 16, 512, 512], P('row', 'head'), may hold values from -6 to 6
- segment_ids: int32 [48, 512], P('row'), may hold values from 0 to 3, never falling along the last dimension, each value on 1 to 320 neighbouring positions
- w_qkv: bfloat16 [1024, 3, 1024], P(None, None, 'head'), may hold values from -0.1875 to 0.1875
- b_qv: bfloat16 [2, 1024], P(None, 'head'), may hold values from -3 to 3
- w_out: bfloat16 [1024, 1024], P('head'), may hold values from -1.5 to 1.5
- b_out: bfloat16 [1024], replicated, may hold values from -3 to 3
- ln1_gain: float32 [1024], replicated, may hold values from 0.5 to 1.5
- ln1_shift: float32 [1024], replicated, may hold values from -2 to 2
- w_in: bfloat16 [1024, 4096], P(None, ('head', 'row')), may hold values from -0.1875 to 0.1875
- b_in: bfloat16 [4096], P(('head', 'row')), may hold values from -3 to 3
- w_down: bfloat16 [4096, 1024], P(('head', 'row')), may hold values from -0.1875 to 0.1875
- b_down: bfloat16 [1024], replicated, may hold values from -2 to 2
- ln2_gain: float32 [1024], replicated, may hold values from 0.5 to 1.5
- ln2_shift: float32 [1024], replicated, may hold values from -2 to 2
- out_grad: bfloat16 [48, 512, 1024], P('row', 'head'), may hold values from -6 to 6
- logit_grad: bfloat16 [48, 16, 512, 512], P('row', 'head'), may hold values from -3 to 3
Outputs:
- layer_out: bfloat16 [48, 512, 1024], P('row', 'head')
- raw_logits: bfloat16 [48, 16, 512, 512], P('row', 'head')
- tokens_grad: float32 [48, 512, 1024], P('row', 'head')
- prev_grad: bfloat16 [48, 16, 512, 512], P('row', 'head')
- grad_w_qkv: float32 [1024, 3, 1024], P(None, None, 'head')
- grad_b_qv: float32 [2, 1024], P(None, 'head')
- grad_w_out: float32 [1024, 1024], P('head')
- grad_b_out: float32 [1024], replicated
- grad_ln1_gain: float32 [1024], replicated
- grad_ln1_shift: float32 [1024], replicated
- grad_w_in: float32 [1024, 4096], P(None, ('head', 'row'))
- grad_b_in: float32 [4096], P(('head', 'row'))
- grad_w_down: float32 [4096, 1024], P(('head', 'row'))
- grad_b_down: float32 [1024], replicated
- grad_ln2_gain: float32 [1024], replicated
- grad_ln2_shift: float32 [1024], replicated
Inputs may be any that keep to these rules, and one draw needn't show every extreme that they name: `segment_ids`: in each row of 512 slots the ids never fall and each id covers 1 to 320 slots.
All inputs are finite; a program needn't handle non-finite values.
Results may differ from a plain program's by a relative error of at most 0.015.
Values may be sent and summed in bfloat16 or wider, within the bound.
No kernel may reach another device: no remote copies, remote signals or barrier semaphores. Data moves between devices by JAX's collectives and lax.ppermute only.
A program may use at most 256 MiB of HBM per device.

v0:
```python
import jax
import jax.numpy as jnp
from jax import lax
from jax.sharding import PartitionSpec as P

norm_eps = 1e-12
masked_fill = -1000000000.0


def layer_norm(values_in, gain_vec, shift_vec):
    center = jnp.mean(values_in, axis=-1, keepdims=True)
    offset = values_in - center
    spread = jnp.mean(offset * offset, axis=-1, keepdims=True)
    inverse = lax.rsqrt(spread + norm_eps)
    unit_vals = offset * inverse
    return (unit_vals * gain_vec + shift_vec, unit_vals, inverse)


def norm_back(grad_in, unit_vals, inverse, gain_vec):
    scaled = grad_in * gain_vec
    return inverse * (
        scaled
        - jnp.mean(scaled, axis=-1, keepdims=True)
        - unit_vals * jnp.mean(scaled * unit_vals, axis=-1, keepdims=True)
    )


def gelu_exact(pre_vals):
    return jax.nn.gelu(pre_vals, approximate=False)


def per_device(
    tokens,
    prev_logits,
    segment_ids,
    w_qkv,
    b_qv,
    w_out,
    b_out,
    ln1_gain,
    ln1_shift,
    w_in,
    b_in,
    w_down,
    b_down,
    ln2_gain,
    ln2_shift,
    out_grad,
    logit_grad,
):
    rows_dev = tokens.shape[0]
    heads_dev = prev_logits.shape[1]
    slots = prev_logits.shape[2]
    head_cols = w_qkv.shape[2]
    head_size = head_cols // heads_dev
    score_scale = head_size ** (-0.5)
    bias_qv = b_qv.astype(jnp.float32)
    bias_full = jnp.stack([bias_qv[0], jnp.zeros_like(bias_qv[0]), bias_qv[1]], axis=0)
    whole_tokens = lax.all_gather(tokens, "head", axis=1, tiled=True)
    projected = jnp.einsum("rsd,dcf->rscf", whole_tokens, w_qkv, preferred_element_type=jnp.float32)
    qkv_low = (projected + bias_full).astype(jnp.bfloat16)
    split_heads = qkv_low.reshape(rows_dev, slots, 3, heads_dev, head_size)
    queries = split_heads[:, :, 0]
    key_rows = split_heads[:, :, 1]
    value_rows = split_heads[:, :, 2]

    def scores_of(query_row, key_row, prev_row, segment_row):
        raw_scores = jnp.einsum(
            "ihe,jhe->hij", query_row, key_row, preferred_element_type=jnp.float32
        ) * score_scale + prev_row.astype(jnp.float32)
        same_doc = segment_row[:, None] == segment_row[None, :]
        return (raw_scores, jnp.where(same_doc[None], raw_scores, masked_fill))

    def attend_row(inputs):
        query_row, key_row, value_row, prev_row, segment_row = inputs
        raw_scores, masked = scores_of(query_row, key_row, prev_row, segment_row)
        row_top = jnp.max(masked, axis=-1, keepdims=True)
        shifted = jnp.exp(masked - row_top)
        totals = jnp.sum(shifted, axis=-1, keepdims=True)
        probs_low = (shifted / totals).astype(jnp.bfloat16)
        context_row = jnp.einsum(
            "hij,jhe->ihe", probs_low, value_row, preferred_element_type=jnp.float32
        )
        return (
            raw_scores.astype(jnp.bfloat16),
            context_row.astype(jnp.bfloat16),
            (row_top + jnp.log(totals))[..., 0],
        )

    raw_logits, context, log_sums = lax.map(
        attend_row, (queries, key_rows, value_rows, prev_logits, segment_ids)
    )
    context_flat = context.reshape(rows_dev, slots, head_cols)
    partial_out = jnp.einsum("rsf,fd->rsd", context_flat, w_out, preferred_element_type=jnp.float32)
    branch = lax.psum_scatter(partial_out, "head", scatter_dimension=1, tiled=True) + b_out.astype(
        jnp.float32
    )
    normed_one, unit_one, inverse_one = layer_norm(
        tokens.astype(jnp.float32) + branch, ln1_gain, ln1_shift
    )
    normed_low = normed_one.astype(jnp.bfloat16)
    full_in, full_down, full_bias = (
        lax.all_gather(w_in, ("head", "row"), axis=1, tiled=True),
        lax.all_gather(w_down, ("head", "row"), axis=0, tiled=True),
        lax.all_gather(b_in, ("head", "row"), axis=0, tiled=True),
    )
    hidden_pre = jnp.einsum(
        "rsd,df->rsf", normed_low, full_in, preferred_element_type=jnp.float32
    ) + full_bias.astype(jnp.float32)
    active_low = gelu_exact(hidden_pre).astype(jnp.bfloat16)
    ffn_out = jnp.einsum(
        "rsf,fd->rsd", active_low, full_down, preferred_element_type=jnp.float32
    ) + b_down.astype(jnp.float32)
    result, unit_two, inverse_two = layer_norm(normed_one + ffn_out, ln2_gain, ln2_shift)
    grad_top = out_grad.astype(jnp.float32)
    grad_two = norm_back(grad_top, unit_two, inverse_two, ln2_gain)
    gain_two_part = jnp.sum(grad_top * unit_two, axis=(0, 1))
    shift_two_part = jnp.sum(grad_top, axis=(0, 1))
    grad_ffn = grad_two.astype(jnp.bfloat16)
    down_part = jnp.sum(grad_ffn.astype(jnp.float32), axis=(0, 1))
    gelu_pull = jax.vjp(gelu_exact, hidden_pre)[1]
    back_in, back_down = (
        lax.all_gather(w_in, ("head", "row"), axis=1, tiled=True),
        lax.all_gather(w_down, ("head", "row"), axis=0, tiled=True),
    )
    grad_active = jnp.einsum("rsd,fd->rsf", grad_ffn, back_down, preferred_element_type=jnp.float32)
    grad_hidden = gelu_pull(grad_active)[0].astype(jnp.bfloat16)
    grad_w_in_full = jnp.einsum(
        "rsd,rsf->df", normed_low, grad_hidden, preferred_element_type=jnp.float32
    )
    grad_w_down_full = jnp.einsum(
        "rsf,rsd->fd", active_low, grad_ffn, preferred_element_type=jnp.float32
    )
    grad_b_in_full = jnp.sum(grad_hidden.astype(jnp.float32), axis=(0, 1))
    grad_w_in, grad_w_down, grad_b_in = (
        lax.psum_scatter(grad_w_in_full, ("head", "row"), scatter_dimension=1, tiled=True),
        lax.psum_scatter(grad_w_down_full, ("head", "row"), scatter_dimension=0, tiled=True),
        lax.psum_scatter(grad_b_in_full, ("head", "row"), scatter_dimension=0, tiled=True),
    )
    grad_one = grad_two + jnp.einsum(
        "rsf,df->rsd", grad_hidden, back_in, preferred_element_type=jnp.float32
    )
    grad_res = norm_back(grad_one, unit_one, inverse_one, ln1_gain)
    gain_one_part = jnp.sum(grad_one * unit_one, axis=(0, 1))
    shift_one_part = jnp.sum(grad_one, axis=(0, 1))
    grad_branch = grad_res.astype(jnp.bfloat16)
    out_bias_part = jnp.sum(grad_branch.astype(jnp.float32), axis=(0, 1))
    whole_grad = lax.all_gather(grad_branch, "head", axis=1, tiled=True)
    grad_w_out_part = jnp.einsum(
        "rsf,rsd->fd", context_flat, whole_grad, preferred_element_type=jnp.float32
    )
    grad_context = jnp.einsum(
        "rsd,fd->rsf", whole_grad, w_out, preferred_element_type=jnp.float32
    ).astype(jnp.bfloat16)
    grad_context = grad_context.reshape(rows_dev, slots, heads_dev, head_size)

    def attend_back(inputs):
        (
            query_row,
            key_row,
            value_row,
            prev_row,
            segment_row,
            log_row,
            grad_ctx_row,
            grad_log_row,
        ) = inputs
        masked = scores_of(query_row, key_row, prev_row, segment_row)[1]
        probs = jnp.exp(masked - log_row[..., None])
        probs_low = probs.astype(jnp.bfloat16)
        grad_value = jnp.einsum(
            "hij,ihe->jhe", probs_low, grad_ctx_row, preferred_element_type=jnp.float32
        )
        grad_probs = jnp.einsum(
            "ihe,jhe->hij", grad_ctx_row, value_row, preferred_element_type=jnp.float32
        )
        inner_sum = jnp.sum(grad_probs * probs, axis=-1, keepdims=True)
        grad_raw = (probs * (grad_probs - inner_sum) + grad_log_row.astype(jnp.float32)).astype(
            jnp.bfloat16
        )
        grad_query = (
            jnp.einsum("hij,jhe->ihe", grad_raw, key_row, preferred_element_type=jnp.float32)
            * score_scale
        )
        grad_key = (
            jnp.einsum("hij,ihe->jhe", grad_raw, query_row, preferred_element_type=jnp.float32)
            * score_scale
        )
        return (
            grad_raw,
            jnp.stack([grad_query, grad_key, grad_value], axis=1).astype(jnp.bfloat16),
        )

    prev_grad, grad_qkv = lax.map(
        attend_back,
        (
            queries,
            key_rows,
            value_rows,
            prev_logits,
            segment_ids,
            log_sums,
            grad_context,
            logit_grad,
        ),
    )
    grad_qkv = grad_qkv.reshape(rows_dev, slots, 3, head_cols)
    grad_w_qkv_part = jnp.einsum(
        "rsd,rscf->dcf", whole_tokens, grad_qkv, preferred_element_type=jnp.float32
    )
    qkv_sums = jnp.sum(grad_qkv.astype(jnp.float32), axis=(0, 1))
    grad_b_qv_part = jnp.stack([qkv_sums[0], qkv_sums[2]], axis=0)
    input_part = jnp.einsum("rscf,dcf->rsd", grad_qkv, w_qkv, preferred_element_type=jnp.float32)
    tokens_grad = grad_res + lax.psum_scatter(
        input_part.astype(jnp.bfloat16), "head", scatter_dimension=1, tiled=True
    ).astype(jnp.float32)
    grad_w_qkv, grad_b_qv, grad_w_out = (
        lax.psum(grad_w_qkv_part.astype(jnp.bfloat16), "row").astype(jnp.float32),
        lax.psum(grad_b_qv_part.astype(jnp.bfloat16), "row").astype(jnp.float32),
        lax.psum(grad_w_out_part.astype(jnp.bfloat16), "row").astype(jnp.float32),
    )
    grad_b_out, grad_ln1_gain, grad_ln1_shift, grad_b_down, grad_ln2_gain, grad_ln2_shift = (
        lax.psum(
            (
                out_bias_part,
                gain_one_part,
                shift_one_part,
                down_part,
                gain_two_part,
                shift_two_part,
            ),
            ("head", "row"),
        )
    )
    return (
        result.astype(jnp.bfloat16),
        raw_logits,
        tokens_grad,
        prev_grad,
        grad_w_qkv,
        grad_b_qv,
        grad_w_out,
        grad_b_out,
        grad_ln1_gain,
        grad_ln1_shift,
        grad_w_in,
        grad_b_in,
        grad_w_down,
        grad_b_down,
        grad_ln2_gain,
        grad_ln2_shift,
    )


def solution(mesh):
    placed = (
        P("row", "head", None),
        P("row", "head", None, None),
        P("row", None),
        P(None, None, "head"),
        P(None, "head"),
        P("head", None),
        P(),
        P(),
        P(),
        P(None, ("head", "row")),
        P(("head", "row")),
        P(("head", "row"), None),
        P(),
        P(),
        P(),
        P("row", "head", None),
        P("row", "head", None, None),
    )
    return jax.shard_map(
        per_device,
        mesh=mesh,
        in_specs=placed,
        out_specs=(
            P("row", "head", None),
            P("row", "head", None, None),
            P("row", "head", None),
            P("row", "head", None, None),
            P(None, None, "head"),
            P(None, "head"),
            P("head", None),
            P(),
            P(),
            P(),
            P(None, ("head", "row")),
            P(("head", "row")),
            P(("head", "row"), None),
            P(),
            P(),
            P(),
        ),
        check_vma=False,
    )
```

profile of v0, /device:TPU:0, one launch (start us, length us, event | category | flops | bytes accessed | tf_op | source)
XLA Modules:
  0.0 1243.4 jit_solution(9460052451162710908)
XLA Ops:
  8.8 17.2 %copy.60 = bf16[6,4,512,512]{2,3,1,0:T(8,128)(2,1)} copy(bf16[6,4,512,512]{3,2,1,0:T(8,128)(2,1)} %param.22) | data formatting | bytes 25165824 | tf_op jit(solution)/shard_map/while | solution.py:90
  26.2 57.4 %all-gather.6.cloned.1.call-done = bf16[6,512,1024]{2,1,0:T(8,128)(2,1)} async-done(((bf16[6,128,1024]{2,1,0:T(8,128)(2,1)}), bf16[6,512,1024]{2,1,0:T(8,128)(2,1)}) %all-gather.6.cloned.1.call-update) | async-done | bytes 6291472 | tf_op jit(solution)/shard_map/all_gather | solution.py:59
  83.6 8.2 add_convert_fusion.1
  99.9 104.8 %while.26 = (s32[]{:T(128)}, bf16[6,4,512,512]{3,2,1,0:T(8,128)(2,1)}, bf16[6,512,4,64]{1,3,2,0:T(8,128)(2,1)}, f32[6,4,512]{2,1,0:T(4,128)S(1)}, bf16[6,512,4,6...) while((s32[]{:T(128)}, ...), condition=%wide.region_3.4_spmd, body=%wide.region_0.3_spmd.sunk | while | flops 282458112 | bytes 60892324 | solution.py:90
  204.7 8.1 fusion.120
  214.1 40.6 %all-gather = bf16[32,1,128]{2,1,0:T(2,128)(2,1)S(1)} all-gather(bf16[1,1,128]{2,1,0:T(2,128)(2,1)S(1)} %bitcast.237), channel_id=1, replica_groups=mesh['head'=4,'row'=8] {'head','row'}, dimensions={0}, use_global_device_ids=true | all-gather | bytes 8448 | tf_op jit(solution)/shard_map/all_gather | solution.py:105
  254.8 95.2 %reduce-scatter.5.cloned.1.call-done = f32[6,128,1024]{2,1,0:T(8,128)} async-done(((f32[6,512,1024]{2,1,0:T(8,128)}), f32[6,128,1024]{2,1,0:T(8,128)}) %reduce-scatter.5.cloned.1.call-update) | async-done | bytes 3145744 | tf_op jit(solution)/shard_map/reduce_scatter | solution.py:95
  355.1 14.5 %fusion.101 = (u8[128,4096]{1,0:T(8,128)(4,1)S(1)}, u8[128,4096]{1,0:T(8,128)(4,1)S(1)}, f32[6,128,4096]{2,1,0:T(8,128)S(1)}) fusion(f32[4096]{0:T(1024)S(1)} %bitcast.234, bf16[1024,4096]{1,0:T(8,128)(2,1)} %all-gather.8.cloned.1.call-done, f32[6,128,1024]{2,1,0:T(8,128)} %copy-done.4, f32[1024]{0:T(1024)S(1)} %copy-done.14, f32[1024]{0:T(1024)S(1)} %copy-done.13, ...), kind=kOutput, calls=%fused_computation.136 | convolution fusion | flops 6489374720 | bytes 25196544 | tf_op jit(solution)/shard_map/rsd,df->rsf/dot_general | solution.py:107
  374.0 30.5 %multiply_convert_fusion = (bf16[6,128,4096]{2,1,0:T(8,128)(2,1)}, f32[6,128,4096]{2,1,0:T(8,128)}) fusion(f32[6,128,4096]{2,1,0:T(8,128)S(1)} %get-tuple-element.279, f32[4096]{0:T(1024)S(1)} %bitcast.235, u8[128,4096]{1,0:T(8,128)(4,1)S(1)} %get-tuple-element.201, u8[128,4096]{1,0:T(8,128)(4,1)S(1)} %get-tuple-element.200), kind=kLoop, calls=%fused_computation.84 | loop fusion | flops 223346688 | bytes 32522240 | tf_op jit(solution)/shard_map/convert_element_type | solution.py:110
  404.5 9.7 all-gather.10.cloned.1.call-done
  414.2 11.8 fusion.131
  433.9 20.5 %convert_reduce_fusion = (f32[4096]{0:T(1024)S(1)}, bf16[6,128,4096]{2,1,0:T(8,128)(2,1)}) fusion(f32[6,128,4096]{2,1,0:T(8,128)} %get-tuple-element.264, bf16[6,128,1024]{2,1,0:T(8,128)(2,1)} %get-tuple-element.260, bf16[4096,1024]{1,0:T(8,128)(2,1)} %all-gather.10.cloned.1.call-done, f32[6,128,4096]{2,1,0:T(8,128)} %copy-done.7, f32[4096]{0:T(1024)S(1)} %bitcast.236), kind=kOutput, calls=%fused_computation.82 | convolution fusion | flops 6495924224 | bytes 41451520 | tf_op jit(solution)/shard_map/rsd,fd->rsf/dot_general | solution.py:126
  454.4 14.6 %multiply_reduce_fusion.1 = (f32[1024]{0:T(1024)S(1)}, f32[6,128]{1,0:T(8,128)S(1)}, f32[6,128]{1,0:T(8,128)S(1)}, f32[1024]{0:T(1024)S(1)}, f32[6,128,1024]{2,1,0:T(8,128)S(1)}) fusion(f32[6,128,1024]{2,1,0:T(8,128)} %copy-done.4, f32[6,128]{1,0:T(8,128)S(1)} %add_rsqrt_fusion.1, f32[6,128]{1,0:T(8,128)S(1)} %broadcast_multiply_fusion.5, ...), kind=kOutput, calls=%fused_computation.124 | convolution fusion | flops 6456602624 | bytes 25731072 | tf_op jit(solution)/shard_map/rsf,df->rsd/dot_general | solution.py:140
  471.3 68.9 %all-gather.12.cloned.1.call-done = bf16[6,512,1024]{2,1,0:T(8,128)(2,1)} async-done(((bf16[6,128,1024]{2,1,0:T(8,128)(2,1)}), bf16[6,512,1024]{2,1,0:T(8,128)(2,1)}) %all-gather.12.cloned.1.call-update) | async-done | bytes 6291472 | tf_op jit(solution)/shard_map/all_gather | solution.py:148
  552.2 210.6 %while.27 = (s32[]{:T(128)}, bf16[6,4,512,512]{3,2,1,0:T(8,128)(2,1)}, bf16[6,512,3,4,64]{1,4,3,2,0:T(8,128)(2,1)}, s32[6,512]{1,0:T(8,128)}, bf16[6,512,4,64]{1...) while((s32[]{:T(128)}, ...), condition=%wide.region_15.16_spmd, body=%wide.region_13.15_spmd.sunk | while | flops 821168640 | bytes 66097308 | solution.py:194
  565.8 7.0 fusion.186
  768.8 8.9 fusion.114
  777.7 9.4 bitcast_convert_fusion
  788.5 13.3 %convolution_bitcast_fusion = f32[4096,1024]{1,0:T(8,128)} fusion(bf16[6,128,4096]{2,1,0:T(8,128)(2,1)} %get-tuple-element.263, bf16[6,128,1024]{2,1,0:T(8,128)(2,1)S(1)} %copy-done.11), kind=kOutput, calls=%fused_computation.98 | convolution fusion | flops 6442450944 | bytes 24641536 | tf_op jit(solution)/shard_map/rsf,rsd->fd/dot_general | solution.py:131
  802.5 13.6 %convolution_bitcast_fusion.1 = f32[1024,4096]{1,0:T(8,128)} fusion(bf16[6,128,4096]{2,1,0:T(8,128)(2,1)} %get-tuple-element.284, f32[6,128,1024]{2,1,0:T(8,128)} %copy-done.4, f32[1024]{0:T(1024)S(1)} %copy-done.15, f32[1024]{0:T(1024)S(1)} %copy-done.13, f32[6,128]{1,0:T(8,128)S(1)} %add_rsqrt_fusion.1, f32[6,128]{1,0:T(8,128)S(1)} %broadcast_multiply_fusion.5), kind=kOutput, calls=%fused_computation.99 | convolution fusion | flops 6446383104 | bytes 26228736 | tf_op jit(solution)/shard_map/rsd,rsf->df/dot_general | solution.py:128
  816.9 40.9 %all-reduce.1 = (f32[1024]{0:T(1024)}, f32[1024]{0:T(1024)}, f32[1024]{0:T(1024)}, f32[4096]{0:T(1024)S(1)}, f32[1024]{0:T(1024)}, /*index=5*/f32[1024]{0:T(1024)}, f32[1024]{0:T(1024)}) all-reduce(f32[1024]{0:T(1024)S(1)} %get-tuple-element.261, f32[1024]{0:T(1024)S(1)} %get-tuple-element.202, ...), channel_id=1, replica_groups=mesh['head'=4,'row'=8] {'head','row'}, use_global_device_ids=true, to_apply=%region_22.23 | all-reduce | flops 10240 | bytes 81920 | tf_op jit(solution)/shard_map/psum | solution.py:223
  861.7 16.0 %psum.64 = bf16[2,256]{1,0:T(2,128)(2,1)S(1)} all-reduce(bf16[2,256]{1,0:T(2,128)(2,1)S(1)} %pad_maximum_fusion.1), channel_id=1, replica_groups=mesh['head'=4,'row'=8] {'row'}, use_global_device_ids=true, to_apply=%region_19.20 | all-reduce | flops 512 | bytes 2048 | tf_op jit(solution)/shard_map/psum | solution.py:219
  887.6 160.6 %reduce-scatter.11.cloned.1.call-done = f32[128,1024]{1,0:T(8,128)} async-done(((f32[4096,1024]{1,0:T(8,128)}), f32[128,1024]{1,0:T(8,128)}) %reduce-scatter.11.cloned.1.call-update) | async-done | bytes 524304 | tf_op jit(solution)/shard_map/reduce_scatter | solution.py:137
  1048.2 187.1 %reduce-scatter.9.cloned.1.call-done = f32[1024,128]{1,0:T(8,128)} async-done(((f32[1024,4096]{1,0:T(8,128)}), f32[1024,128]{1,0:T(8,128)}) %reduce-scatter.9.cloned.1.call-update) | async-done | bytes 524304 | tf_op jit(solution)/shard_map/reduce_scatter | solution.py:136
  (263 shorter events, 372.0 us)
Async XLA Ops:
  8.0 75.6 %copy-start = (bf16[1024,3,256]{2,0,1:T(8,128)(2,1)S(1)}, bf16[1024,3,256]{2,0,1:T(8,128)(2,1)}, u32[]{:S(2)}) copy-start(bf16[1024,3,256]{2,0,1:T(8,128)(2,1)} %param.24) | copy-start | bytes 4718596
  8.0 75.6 %all-gather.6.cloned.1.call-start = ((), (), s32[]{:S(2)}) async-start(), calls=%async_computation.4 | async-start | bytes 7864320 | tf_op jit(solution)/shard_map/all_gather | solution.py:59
  8.8 341.3 %reduce-scatter.5.cloned.1.call-start = ((), (), s32[]{:S(2)}) async-start(), calls=%async_computation.5 | async-start | bytes 15728640 | tf_op jit(solution)/shard_map/reduce_scatter | solution.py:95
  8.8 17.3 %copy-start.21 = (bf16[2,256]{1,0:T(2,128)(2,1)S(1)}, bf16[2,256]{1,0:T(2,128)(2,1)}, u32[]{:S(2)}) copy-start(bf16[2,256]{1,0:T(2,128)(2,1)} %param.25) | copy-start | bytes 3076
  212.8 41.9 %copy-start.23 = (bf16[1024]{0:T(1024)(128)(2,1)S(1)}, bf16[1024]{0:T(1024)(128)(2,1)}, u32[]{:S(2)}) copy-start(bf16[1024]{0:T(1024)(128)(2,1)} %param.33) | copy-start | bytes 6148
  212.9 142.2 %all-gather.8.cloned.1.call-start = ((), (), s32[]{:S(2)}) async-start(), calls=%async_computation.6 | async-start | bytes 8650752 | tf_op jit(solution)/shard_map/all_gather | solution.py:103
  213.5 200.7 %all-gather.10.cloned.1.call-start = ((), (), s32[]{:S(2)}) async-start(), calls=%async_computation.7 | async-start | bytes 8650752 | tf_op jit(solution)/shard_map/all_gather | solution.py:104
  214.0 326.2 %all-gather.12.cloned.1.call-start = ((), (), s32[]{:S(2)}) async-start(), calls=%async_computation.8 | async-start | bytes 7864320 | tf_op jit(solution)/shard_map/all_gather | solution.py:148
  254.8 100.3 %copy-start.13 = (f32[1024]{0:T(1024)S(1)}, f32[1024]{0:T(1024)}, u32[]{:S(2)}) copy-start(f32[1024]{0:T(1024)} %param.28) | copy-start | bytes 12292
  254.8 100.3 %copy-start.14 = (f32[1024]{0:T(1024)S(1)}, f32[1024]{0:T(1024)}, u32[]{:S(2)}) copy-start(f32[1024]{0:T(1024)} %param.29) | copy-start | bytes 12292
  414.2 12.4 copy-start.17
  426.0 7.9 copy-start.6
  454.4 14.7 %copy-start.5 = (f32[6,128,1024]{2,1,0:T(8,128)S(1)}, f32[6,128,1024]{2,1,0:T(8,128)}, u32[]{:S(2)}) copy-start(f32[6,128,1024]{2,1,0:T(8,128)} %copy-done.4) | copy-start | bytes 9437188
  471.3 407.0 %all-reduce.5.cloned.1.call-start = ((), (), s32[]{:S(2)}) async-start(), calls=%async_computation.12 | async-start | bytes 4194304 | tf_op jit(solution)/shard_map/psum | solution.py:218
  572.9 4.7 copy-start.3
  607.9 4.7 copy-start.3
  643.0 4.7 copy-start.3
  678.0 4.7 copy-start.3
  713.1 4.7 copy-start.3
  748.1 4.7 copy-start.3
  762.8 6.0 copy-start.10
  777.6 104.9 %reduce-scatter.7.cloned.1.call-start = ((), (), s32[]{:S(2)}) async-start(), calls=%async_computation.9 | async-start | bytes 7864320 | tf_op jit(solution)/shard_map/reduce_scatter | solution.py:214
  787.1 261.1 %reduce-scatter.11.cloned.1.call-start = ((), (), s32[]{:S(2)}) async-start(), calls=%async_computation.11 | async-start | bytes 17301504 | tf_op jit(solution)/shard_map/reduce_scatter | solution.py:137
  801.9 433.5 %reduce-scatter.9.cloned.1.call-start = ((), (), s32[]{:S(2)}) async-start(), calls=%async_computation.10 | async-start | bytes 17301504 | tf_op jit(solution)/shard_map/reduce_scatter | solution.py:136
  (25 other events, 56.7 us)
Sparse Core Ops, SparseCore 0:
  10.7 72.8 all-gather.5
  213.0 136.9 reduce-scatter.4
  471.4 68.7 all-gather.11
  787.2 71.5 reduce-scatter.6
  861.5 186.6 reduce-scatter.10
  1051.0 184.3 reduce-scatter.8
Sparse Core Ops, SparseCore 1:
  216.2 116.3 all-gather.7
  335.4 78.7 all-gather.9
  777.7 65.6 all-reduce.4
where the time goes:
time: 1250 us; the launch traced here: 1240 us
  waiting for transfers between devices  581 us (46%)
  matrix products  277 us (22%)
  local copies, waits for them, and re-layouts  197 us (16%)
  blocking collectives  97.5 us (8%)
  other arithmetic  73 us (6%)
  between operations  16.5 us (1%)
    reduce_scatter x1, waiting for transfers between devices, per_device(): lax.psum_scatter(grad_w_in_full, ('head', 'row'), scatter_dimension=1, ti...  187 us
    reduce_scatter x1, waiting for transfers between devices, per_device(): lax.psum_scatter(grad_w_down_full, ('head', 'row'), scatter_dimension=0,...  161 us
    reduce_scatter x1, waiting for transfers between devices, per_device(): lax.psum_scatter(partial_out, 'head', scatter_dimension=1, tiled=True)  95.2 us
    dynamic_update_slice x24, local copies, waits for them, and re-layouts, per_device(): lax.map(attend_row, (queries, key_rows, value_rows, prev_logits, segment_...  87.1 us
    all_gather x1, waiting for transfers between devices, per_device(): whole_grad = lax.all_gather(grad_branch, 'head', axis=1, tiled=True)  68.9 us
    all_gather x1, waiting for transfers between devices, per_device(): whole_tokens = lax.all_gather(tokens, 'head', axis=1, tiled=True)  57.4 us
    dynamic_slice x24, local copies, waits for them, and re-layouts, per_device(): lax.map(attend_row, (queries, key_rows, value_rows, prev_logits, segment_...  51.7 us
    dot_general x12, matrix products, scores_of(): jnp.einsum('ihe,jhe->hij', query_row, key_row, preferred_element_type=jnp...  50 us
  transfers between devices with their start and end apart: 9, of which 6 were waited for; matrix products, arithmetic and copies ran while one was open for 9% of the time, Pallas kernels for 0%

commit v1 on v0

v1 whole, which is shorter than its diff:
```python
import functools

import jax
import jax.numpy as jnp
from jax import lax
from jax.experimental import pallas as pl
from jax.experimental.pallas import tpu as pltpu
from jax.sharding import PartitionSpec as P

norm_eps = 1e-12
masked_fill = -1000000000.0
head_dim = 64
hidden_block = 512
bf16 = jnp.bfloat16
f32 = jnp.float32


def dot_nn(a, b):
    return lax.dot_general(a, b, (((1,), (0,)), ((), ())), preferred_element_type=f32)


def dot_nt(a, b):
    return lax.dot_general(a, b, (((1,), (1,)), ((), ())), preferred_element_type=f32)


def dot_tn(a, b):
    return lax.dot_general(a, b, (((0,), (0,)), ((), ())), preferred_element_type=f32)


def params(limit_mib=60):
    return pltpu.CompilerParams(
        dimension_semantics=("arbitrary",), vmem_limit_bytes=limit_mib * 1024 * 1024
    )


def whole(shape):
    return pl.BlockSpec(shape, lambda *_: (0,) * len(shape))


def by_step(shape, axis=0):
    return pl.BlockSpec(shape, lambda t, *_: tuple(t if d == axis else 0 for d in range(len(shape))))


def norm_parts(values):
    center = jnp.mean(values, axis=-1, keepdims=True)
    offset = values - center
    inverse = lax.rsqrt(jnp.mean(offset * offset, axis=-1, keepdims=True) + norm_eps)
    return offset * inverse, inverse


def norm_back(grad_in, unit_vals, inverse, gain_vec):
    scaled = grad_in * gain_vec
    return inverse * (
        scaled
        - jnp.mean(scaled, axis=-1, keepdims=True)
        - unit_vals * jnp.mean(scaled * unit_vals, axis=-1, keepdims=True)
    )


def lane_halves():
    lane = lax.broadcasted_iota(jnp.int32, (1, 2 * head_dim), 1)
    return lane < head_dim


def attend(me, tok_pieces, w_flat, bias_row, seg_row, seg_col, prev):
    rows, heads, slots, _ = prev.shape
    nh = len(tok_pieces)
    _, part, width = tok_pieces[0].shape
    cols = heads * head_dim
    step = 128
    scale = head_dim ** (-0.5)

    def body(me_ref, *refs):
        toks = refs[:nh]
        w_ref, b_ref, sr_ref, sc_ref, prev_ref = refs[nh : nh + 5]
        qkv_ref, raw_ref, ctx_ref, lse_ref, tok_all, ctx_all = refs[nh + 5 :]
        mine = me_ref[0]
        for k in range(nh):
            tok_all[pl.ds(pl.multiple_of((mine ^ k) * part, part), part), :] = toks[k][0]
        qkv_ref[0] = (dot_nn(tok_all[...], w_ref[...]) + b_ref[...]).astype(bf16)
        low_half = lane_halves()
        keep = [jnp.where(low_half, scale, 0.0).astype(bf16), jnp.where(low_half, 0.0, scale).astype(bf16)]
        lane = lax.broadcasted_iota(jnp.int32, (step, 128), 1)

        def block(i, carry):
            at = pl.ds(pl.multiple_of(i * step, step), step)
            same = sc_ref[0, at, :] == sr_ref[0]
            lse_tile = jnp.zeros((step, 128), f32)
            for pair in range(heads // 2):
                span = slice(pair * 128, pair * 128 + 128)
                q_pair = qkv_ref[0, at, span]
                k_pair = qkv_ref[0, :, cols + pair * 128 : cols + pair * 128 + 128]
                v_pair = qkv_ref[0, :, 2 * cols + pair * 128 : 2 * cols + pair * 128 + 128]
                outs = []
                for half in range(2):
                    h = 2 * pair + half
                    raw = dot_nt(q_pair * keep[half], k_pair) + prev_ref[0, h, at, :].astype(f32)
                    raw_ref[0, h, at, :] = raw.astype(bf16)
                    masked = jnp.where(same, raw, masked_fill)
                    top = jnp.max(masked, axis=-1, keepdims=True)
                    grown = jnp.exp(masked - top)
                    total = jnp.sum(grown, axis=-1, keepdims=True)
                    probs = (grown * (1.0 / total)).astype(bf16)
                    outs.append(dot_nn(probs, v_pair))
                    lse_tile = jnp.where(lane == h, top + jnp.log(total), lse_tile)
                ctx_all[at, span] = jnp.where(low_half, outs[0], outs[1]).astype(bf16)
            lse_ref[0, at, :] = lse_tile
            return carry

        lax.fori_loop(0, slots // step, block, 0)
        for k in range(nh):
            ctx_ref[k, 0] = ctx_all[pl.ds(pl.multiple_of((mine ^ k) * part, part), part), :]

    return pl.pallas_call(
        body,
        grid_spec=pltpu.PrefetchScalarGridSpec(
            num_scalar_prefetch=1,
            grid=(rows,),
            in_specs=[by_step((1, part, width))] * nh
            + [
                whole((width, 3 * cols)),
                whole((1, 3 * cols)),
                by_step((1, 1, slots)),
                by_step((1, slots, 1)),
                by_step((1, heads, slots, slots)),
            ],
            out_specs=[
                by_step((1, slots, 3 * cols)),
                by_step((1, heads, slots, slots)),
                by_step((nh, 1, part, cols), 1),
                by_step((1, slots, 128)),
            ],
            scratch_shapes=[pltpu.VMEM((slots, width), bf16), pltpu.VMEM((slots, cols), bf16)],
        ),
        out_shape=[
            jax.ShapeDtypeStruct((rows, slots, 3 * cols), bf16),
            jax.ShapeDtypeStruct((rows, heads, slots, slots), bf16),
            jax.ShapeDtypeStruct((nh, rows, part, cols), bf16),
            jax.ShapeDtypeStruct((rows, slots, 128), f32),
        ],
        compiler_params=params(),
        name="attend",
    )(me, *tok_pieces, w_flat, bias_row, seg_row, seg_col, prev)


def attend_back(me, tok_pieces, ctx_grads, qkv, prev, logit_grad, seg_row, seg_col, lse, w_flat):
    rows, heads, slots, _ = prev.shape
    nh = len(tok_pieces)
    _, part, width = tok_pieces[0].shape
    cols = heads * head_dim
    step = 128
    scale = head_dim ** (-0.5)

    def body(me_ref, *refs):
        toks, grads = refs[:nh], refs[nh : 2 * nh]
        qkv_ref, prev_ref, lg_ref, sr_ref, sc_ref, lse_ref, w_ref = refs[2 * nh : 2 * nh + 7]
        pg_ref, in_ref, gw_ref, gb_ref, tok_all, go_all, p_all, dt_all, in_all = refs[2 * nh + 7 :]
        mine = me_ref[0]
        for k in range(nh):
            at = pl.ds(pl.multiple_of((mine ^ k) * part, part), part)
            tok_all[at, :] = toks[k][0]
            go_all[at, :] = grads[k][0]
        low_half = lane_halves()
        keep_q = [jnp.where(low_half, scale, 0.0).astype(bf16), jnp.where(low_half, 0.0, scale).astype(bf16)]
        keep_g = [jnp.where(low_half, 1.0, 0.0).astype(bf16), jnp.where(low_half, 0.0, 1.0).astype(bf16)]

        def block(i, carry):
            at = pl.ds(pl.multiple_of(i * step, step), step)
            same = sc_ref[0, at, :] == sr_ref[0]
            lse_tile = lse_ref[0, at, :]
            for pair in range(heads // 2):
                span = slice(pair * 128, pair * 128 + 128)
                q_pair = qkv_ref[0, at, span]
                g_pair = go_all[at, span]
                k_pair = qkv_ref[0, :, cols + pair * 128 : cols + pair * 128 + 128]
                v_pair = qkv_ref[0, :, 2 * cols + pair * 128 : 2 * cols + pair * 128 + 128]
                for half in range(2):
                    h = 2 * pair + half
                    raw = dot_nt(q_pair * keep_q[half], k_pair) + prev_ref[0, h, at, :].astype(f32)
                    probs = jnp.exp(jnp.where(same, raw, masked_fill) - lse_tile[:, h : h + 1])
                    p_all[h, at, :] = probs.astype(bf16)
                    pulled = probs * dot_nt(g_pair * keep_g[half], v_pair)
                    inner = jnp.sum(pulled, axis=-1, keepdims=True)
                    pg_ref[0, h, at, :] = (pulled - probs * inner + lg_ref[0, h, at, :].astype(f32)).astype(bf16)
            return carry

        lax.fori_loop(0, slots // step, block, 0)
        q_t = qkv_ref[0, :, :cols].T
        k_t = qkv_ref[0, :, cols : 2 * cols].T
        g_t = go_all[...].T
        for h in range(heads):
            span = slice(h * head_dim, h * head_dim + head_dim)
            grad_raw = pg_ref[0, h]
            dt_all[h * head_dim : (h + 1) * head_dim, :] = (dot_nt(k_t[span], grad_raw) * scale).astype(bf16)
            dt_all[cols + h * head_dim : cols + (h + 1) * head_dim, :] = (dot_nn(q_t[span], grad_raw) * scale).astype(bf16)
            dt_all[2 * cols + h * head_dim : 2 * cols + (h + 1) * head_dim, :] = dot_nn(g_t[span], p_all[h]).astype(bf16)
        grad_qkv = dt_all[...].T
        in_all[...] = dot_nt(grad_qkv, w_ref[...]).astype(bf16)
        for k in range(nh):
            in_ref[k, 0] = in_all[pl.ds(pl.multiple_of((mine ^ k) * part, part), part), :]
        gw = dot_nn(dt_all[...], tok_all[...])
        gb = dot_nn(jnp.ones((8, slots), bf16), grad_qkv)

        @pl.when(pl.program_id(0) == 0)
        def _():
            gw_ref[...] = gw
            gb_ref[...] = gb

        @pl.when(pl.program_id(0) > 0)
        def _():
            gw_ref[...] += gw
            gb_ref[...] += gb

    return pl.pallas_call(
        body,
        grid_spec=pltpu.PrefetchScalarGridSpec(
            num_scalar_prefetch=1,
            grid=(rows,),
            in_specs=[by_step((1, part, width))] * nh
            + [by_step((1, part, cols))] * nh
            + [
                by_step((1, slots, 3 * cols)),
                by_step((1, heads, slots, slots)),
                by_step((1, heads, slots, slots)),
                by_step((1, 1, slots)),
                by_step((1, slots, 1)),
                by_step((1, slots, 128)),
                whole((width, 3 * cols)),
            ],
            out_specs=[
                by_step((1, heads, slots, slots)),
                by_step((nh, 1, part, width), 1),
                whole((3 * cols, width)),
                whole((8, 3 * cols)),
            ],
            scratch_shapes=[
                pltpu.VMEM((slots, width), bf16),
                pltpu.VMEM((slots, cols), bf16),
                pltpu.VMEM((heads, slots, slots), bf16),
                pltpu.VMEM((3 * cols, slots), bf16),
                pltpu.VMEM((slots, width), bf16),
            ],
        ),
        out_shape=[
            jax.ShapeDtypeStruct((rows, heads, slots, slots), bf16),
            jax.ShapeDtypeStruct((nh, rows, part, width), bf16),
            jax.ShapeDtypeStruct((3 * cols, width), f32),
            jax.ShapeDtypeStruct((8, 3 * cols), f32),
        ],
        compiler_params=params(),
        name="attend_back",
    )(me, *tok_pieces, *ctx_grads, qkv, prev, logit_grad, seg_row, seg_col, lse, w_flat)


def weight_stream(refs, counts, per_block, buf, sem):
    total = sum(counts)
    t = pl.program_id(0)

    def start(which):
        low = 0
        for ref, count in zip(refs, counts):

            @pl.when((which >= low) & (which < low + count))
            def _(ref=ref, low=low):
                pltpu.make_async_copy(
                    ref.at[pl.ds((which - low) * per_block, per_block)], buf.at[which % 2], sem.at[which % 2]
                ).start()

            low += count

    @pl.when(t == 0)
    def _():
        start(t)

    pltpu.make_async_copy(refs[0].at[pl.ds(0, per_block)], buf.at[t % 2], sem.at[t % 2]).wait()

    @pl.when(t + 1 < total)
    def _():
        start(t + 1)

    return t % 2


def feed_forward(ctx_pieces, out_pieces, tokens, vectors, bias_blocks, weights, out_grad):
    count, width = tokens.shape
    nh = len(ctx_pieces)
    cols = ctx_pieces[0].shape[1]
    shard = weights[0].shape[2]
    per_block = hidden_block // shard
    counts = [w.shape[0] // per_block for w in weights]
    blocks = sum(counts)
    hidden = blocks * hidden_block
    tile = count // 3
    nw = len(weights)

    def body(*refs):
        ctx, outs = refs[:nh], refs[nh : 2 * nh]
        tok_ref, vec_ref, bias_ref, og_ref = refs[2 * nh : 2 * nh + 4]
        w_refs = refs[2 * nh + 4 : 2 * nh + 4 + nw]
        res_ref, x_ref, unit_ref, inv_ref, g2_ref, gf_ref, act_ref, slope_ref, sum_ref = refs[
            2 * nh + 4 + nw : 2 * nh + 13 + nw
        ]
        nrm, acc, buf, sem = refs[2 * nh + 13 + nw :]
        t = pl.program_id(0)
        slot = weight_stream(w_refs, counts, per_block, buf, sem)

        @pl.when(t == 0)
        def _():
            branch = vec_ref[0:1, :] + dot_nn(ctx[0][...], outs[0][...])
            for k in range(1, nh):
                branch = branch + dot_nn(ctx[k][...], outs[k][...])
            unit_one, inverse = norm_parts(tok_ref[...].astype(f32) + branch)
            unit_ref[...] = unit_one
            inv_ref[...] = jnp.broadcast_to(inverse, (count, 128))
            normed = unit_one * vec_ref[1:2, :] + vec_ref[2:3, :]
            nrm[...] = normed
            x_ref[...] = normed.astype(bf16)
            acc[...] = jnp.zeros_like(acc)

        w_in = buf[slot, :, 0].reshape(hidden_block, width)
        w_down = buf[slot, :, 1].reshape(hidden_block, width)
        for m in range(3):
            at = slice(m * tile, m * tile + tile)
            pre = dot_nt(x_ref[at, :], w_in) + bias_ref[0]
            below = 0.5 * (1.0 + lax.erf(pre * (0.5**0.5)))
            active = (pre * below).astype(bf16)
            act_ref[at, :] = active
            slope_ref[at, :] = (below + pre * (jnp.exp(-0.5 * pre * pre) * 0.3989422804014327)).astype(bf16)
            acc[at, :] += dot_nn(active, w_down)

        @pl.when(t == blocks - 1)
        def _():
            unit_two, inverse = norm_parts(nrm[...] + acc[...] + vec_ref[3:4, :])
            res_ref[...] = (unit_two * vec_ref[4:5, :] + vec_ref[5:6, :]).astype(bf16)
            top = og_ref[...].astype(f32)
            grad_two = norm_back(top, unit_two, inverse, vec_ref[4:5, :])
            g2_ref[...] = grad_two
            low = grad_two.astype(bf16)
            gf_ref[...] = low
            sum_ref[0:1, :] = jnp.sum(top * unit_two, axis=0, keepdims=True)
            sum_ref[1:2, :] = jnp.sum(top, axis=0, keepdims=True)
            sum_ref[2:3, :] = jnp.sum(low.astype(f32), axis=0, keepdims=True)
            sum_ref[3:8, :] = jnp.zeros((5, width), f32)

    return pl.pallas_call(
        body,
        grid=(blocks,),
        in_specs=[whole((count, cols))] * nh
        + [whole((cols, width))] * nh
        + [whole((count, width)), whole((8, width)), by_step((1, 1, hidden_block)), whole((count, width))]
        + [pl.BlockSpec(memory_space=pl.ANY)] * nw,
        out_specs=[
            whole((count, width)),
            whole((count, width)),
            whole((count, width)),
            whole((count, 128)),
            whole((count, width)),
            whole((count, width)),
            by_step((count, hidden_block), 1),
            by_step((count, hidden_block), 1),
            whole((8, width)),
        ],
        out_shape=[
            jax.ShapeDtypeStruct((count, width), bf16),
            jax.ShapeDtypeStruct((count, width), bf16),
            jax.ShapeDtypeStruct((count, width), f32),
            jax.ShapeDtypeStruct((count, 128), f32),
            jax.ShapeDtypeStruct((count, width), f32),
            jax.ShapeDtypeStruct((count, width), bf16),
            jax.ShapeDtypeStruct((count, hidden), bf16),
            jax.ShapeDtypeStruct((count, hidden), bf16),
            jax.ShapeDtypeStruct((8, width), f32),
        ],
        scratch_shapes=[
            pltpu.VMEM((count, width), f32),
            pltpu.VMEM((count, width), f32),
            pltpu.VMEM((2, per_block, 2, shard, width), bf16),
            pltpu.SemaphoreType.DMA((2,)),
        ],
        compiler_params=params(),
        name="feed_forward",
    )(*ctx_pieces, *out_pieces, tokens, vectors, bias_blocks, out_grad, *weights)


def feed_back(ctx_pieces, out_pieces, grad_two, grad_ffn, slope, unit_one, inv_one, vectors, weights):
    count, width = grad_two.shape
    nh = len(ctx_pieces)
    cols = ctx_pieces[0].shape[1]
    shard = weights[0].shape[2]
    per_block = hidden_block // shard
    counts = [w.shape[0] // per_block for w in weights]
    blocks = sum(counts)
    hidden = blocks * hidden_block
    tile = count // 3
    nw = len(weights)

    def body(*refs):
        ctx, outs = refs[:nh], refs[nh : 2 * nh]
        g2_ref, gf_ref, slope_ref, unit_ref, inv_ref, vec_ref = refs[2 * nh : 2 * nh + 6]
        w_refs = refs[2 * nh + 6 : 2 * nh + 6 + nw]
        res_ref, gc_ref, gwo_ref, gh_ref, gb_ref, sum_ref, acc, buf, sem = refs[2 * nh + 6 + nw :]
        t = pl.program_id(0)
        slot = weight_stream(w_refs, counts, per_block, buf, sem)

        @pl.when(t == 0)
        def _():
            acc[...] = g2_ref[...]

        w_in = buf[slot, :, 0].reshape(hidden_block, width)
        w_down = buf[slot, :, 1].reshape(hidden_block, width)
        total = jnp.zeros((1, hidden_block), f32)
        for m in range(3):
            at = slice(m * tile, m * tile + tile)
            grad_hidden = (dot_nt(gf_ref[at, :], w_down) * slope_ref[at, :].astype(f32)).astype(bf16)
            gh_ref[at, :] = grad_hidden
            total = total + jnp.sum(grad_hidden.astype(f32), axis=0, keepdims=True)
            acc[at, :] += dot_nn(grad_hidden, w_in)
        gb_ref[0] = total

        @pl.when(t == blocks - 1)
        def _():
            grad_one = acc[...]
            unit_one = unit_ref[...]
            grad_res = norm_back(grad_one, unit_one, inv_ref[:, 0:1], vec_ref[1:2, :])
            res_ref[...] = grad_res
            low = grad_res.astype(bf16)
            sum_ref[0:1, :] = jnp.sum(grad_one * unit_one, axis=0, keepdims=True)
            sum_ref[1:2, :] = jnp.sum(grad_one, axis=0, keepdims=True)
            sum_ref[2:3, :] = jnp.sum(low.astype(f32), axis=0, keepdims=True)
            sum_ref[3:8, :] = jnp.zeros((5, width), f32)
            for k in range(nh):
                gc_ref[k] = dot_nt(low, outs[k][...]).astype(bf16)
                gwo_ref[k] = dot_tn(ctx[k][...], low).astype(bf16)

    return pl.pallas_call(
        body,
        grid=(blocks,),
        in_specs=[whole((count, cols))] * nh
        + [whole((cols, width))] * nh
        + [
            whole((count, width)),
            whole((count, width)),
            by_step((count, hidden_block), 1),
            whole((count, width)),
            whole((count, 128)),
            whole((8, width)),
        ]
        + [pl.BlockSpec(memory_space=pl.ANY)] * nw,
        out_specs=[
            whole((count, width)),
            whole((nh, count, cols)),
            whole((nh, cols, width)),
            by_step((count, hidden_block), 1),
            by_step((1, 1, hidden_block)),
            whole((8, width)),
        ],
        out_shape=[
            jax.ShapeDtypeStruct((count, width), f32),
            jax.ShapeDtypeStruct((nh, count, cols), bf16),
            jax.ShapeDtypeStruct((nh, cols, width), bf16),
            jax.ShapeDtypeStruct((count, hidden), bf16),
            jax.ShapeDtypeStruct((blocks, 1, hidden_block), f32),
            jax.ShapeDtypeStruct((8, width), f32),
        ],
        scratch_shapes=[
            pltpu.VMEM((count, width), f32),
            pltpu.VMEM((2, per_block, 2, shard, width), bf16),
            pltpu.SemaphoreType.DMA((2,)),
        ],
        compiler_params=params(),
        name="feed_back",
    )(*ctx_pieces, *out_pieces, grad_two, grad_ffn, slope, unit_one, inv_one, vectors, *weights)


def weight_grads(x_low, grad_ffn, grad_hidden, active, first, blocks, shard):
    count, width = x_low.shape
    per_block = hidden_block // shard

    def body(x_ref, gf_ref, gh_ref, act_ref, out_ref):
        out_ref[:, 0] = dot_tn(gh_ref[...], x_ref[...]).astype(bf16).reshape(per_block, shard, width)
        out_ref[:, 1] = dot_tn(act_ref[...], gf_ref[...]).astype(bf16).reshape(per_block, shard, width)

    return pl.pallas_call(
        body,
        grid=(blocks,),
        in_specs=[
            whole((count, width)),
            whole((count, width)),
            pl.BlockSpec((count, hidden_block), lambda t: (0, first + t)),
            pl.BlockSpec((count, hidden_block), lambda t: (0, first + t)),
        ],
        out_specs=by_step((per_block, 2, shard, width)),
        out_shape=jax.ShapeDtypeStruct((blocks * per_block, 2, shard, width), bf16),
        compiler_params=params(),
        name="weight_grads",
    )(x_low, grad_ffn, grad_hidden, active)


def per_device(
    nh,
    tokens,
    prev_logits,
    segment_ids,
    w_qkv,
    b_qv,
    w_out,
    b_out,
    ln1_gain,
    ln1_shift,
    w_in,
    b_in,
    w_down,
    b_down,
    ln2_gain,
    ln2_shift,
    out_grad,
    logit_grad,
):
    rows, part, width = tokens.shape
    heads = prev_logits.shape[1]
    slots = prev_logits.shape[2]
    cols = heads * head_dim
    shard = w_in.shape[1]
    count = rows * part
    me = lax.axis_index("head").astype(jnp.int32).reshape(1)

    def swap(value, k):
        return lax.ppermute(value, "head", [(i, i ^ k) for i in range(nh)])

    tok_pieces = [tokens] + [swap(tokens, k) for k in range(1, nh)]
    out_pieces = [w_out] + [swap(w_out, k) for k in range(1, nh)]
    weights = lax.all_gather(jnp.stack([w_in.T, w_down])[None], ("head", "row"), axis=0, tiled=True)
    bias_all = lax.all_gather(b_in.astype(f32), ("head", "row"), axis=0, tiled=True)
    bias_blocks = bias_all.reshape(-1, 1, hidden_block)
    blocks = bias_blocks.shape[0]
    vectors = jnp.stack(
        [
            b_out.astype(f32),
            ln1_gain,
            ln1_shift,
            b_down.astype(f32),
            ln2_gain,
            ln2_shift,
            jnp.zeros_like(ln1_gain),
            jnp.zeros_like(ln1_gain),
        ]
    )
    bias_qv = b_qv.astype(f32)
    bias_row = jnp.concatenate([bias_qv[0], jnp.zeros_like(bias_qv[0]), bias_qv[1]])[None]
    w_flat = w_qkv.reshape(width, 3 * cols)
    seg_row = segment_ids[:, None, :]
    seg_col = segment_ids[:, :, None]

    qkv, raw_logits, ctx, lse = attend(me, tok_pieces, w_flat, bias_row, seg_row, seg_col, prev_logits)
    ctx = ctx.reshape(nh, count, cols)
    ctx_pieces = [ctx[0]] + [swap(ctx[k], k) for k in range(1, nh)]
    flat_tokens = tokens.reshape(count, width)
    layer_out, x_low, unit_one, inv_one, grad_two, grad_ffn, active, slope, sums_two = feed_forward(
        ctx_pieces, out_pieces, flat_tokens, vectors, bias_blocks, [weights], out_grad.reshape(count, width)
    )
    grad_res, ctx_grad, gwo, grad_hidden, gb_in, sums_one = feed_back(
        ctx_pieces, out_pieces, grad_two, grad_ffn, slope, unit_one, inv_one, vectors, [weights]
    )
    ctx_grad = ctx_grad.reshape(nh, rows, part, cols)
    ctx_grads = [ctx_grad[0]] + [swap(ctx_grad[k], k) for k in range(1, nh)]
    ffn_grads = weight_grads(x_low, grad_ffn, grad_hidden, active, 0, blocks, shard)
    own_grads = lax.psum_scatter(ffn_grads, ("head", "row"), scatter_dimension=0, tiled=True)

    prev_grad, input_part, gw, gb = attend_back(
        me, tok_pieces, ctx_grads, qkv, prev_logits, logit_grad, seg_row, seg_col, lse, w_flat
    )
    received = [swap(input_part[k], k).astype(f32) for k in range(1, nh)]
    tokens_grad = grad_res.reshape(rows, part, width) + input_part[0].astype(f32)
    for piece in received:
        tokens_grad = tokens_grad + piece
    gwo_sum = gwo[0].astype(f32)
    for k in range(1, nh):
        gwo_sum = gwo_sum + swap(gwo[k], k).astype(f32)
    grad_w_qkv, grad_w_out = lax.psum((gw.T.astype(bf16), gwo_sum.astype(bf16)), "row")
    grad_w_qkv = grad_w_qkv.astype(f32).reshape(width, 3, cols)
    grad_b_qv = lax.psum(jnp.stack([gb[0, :cols], gb[0, 2 * cols :]]), "row")
    totals, grad_b_in = lax.psum(
        (jnp.concatenate([sums_two[:3], sums_one[:3]]), gb_in.reshape(-1)), ("head", "row")
    )
    place = lax.axis_index(("head", "row"))
    grad_b_in = lax.dynamic_slice_in_dim(grad_b_in, place * shard, shard)
    return (
        layer_out.reshape(rows, part, width),
        raw_logits,
        tokens_grad,
        prev_grad,
        grad_w_qkv,
        grad_b_qv,
        grad_w_out.astype(f32),
        totals[5],
        totals[3],
        totals[4],
        own_grads[0, 0].astype(f32).T,
        grad_b_in,
        own_grads[0, 1].astype(f32),
        totals[2],
        totals[0],
        totals[1],
    )


def solution(mesh):
    placed = (
        P("row", "head", None),
        P("row", "head", None, None),
        P("row", None),
        P(None, None, "head"),
        P(None, "head"),
        P("head", None),
        P(),
        P(),
        P(),
        P(None, ("head", "row")),
        P(("head", "row")),
        P(("head", "row"), None),
        P(),
        P(),
        P(),
        P("row", "head", None),
        P("row", "head", None, None),
    )
    return jax.shard_map(
        functools.partial(per_device, mesh.shape["head"]),
        mesh=mesh,
        in_specs=placed,
        out_specs=(
            P("row", "head", None),
            P("row", "head", None, None),
            P("row", "head", None),
            P("row", "head", None, None),
            P(None, None, "head"),
            P(None, "head"),
            P("head", None),
            P(),
            P(),
            P(),
            P(None, ("head", "row")),
            P(("head", "row")),
            P(("head", "row"), None),
            P(),
            P(),
            P(),
        ),
        check_vma=False,
    )
```

time: 1250 us -> 631 us (0.50)
  waiting for transfers between devices: 581 us -> 184 us
  matrix products: 277 us -> 0 us
  Pallas kernels: 0 us -> 183 us
  local copies, waits for them, and re-layouts: 197 us -> 28 us
  blocking collectives: 97.5 us -> 182 us
  other arithmetic: 73 us -> 17.5 us
  starting transfers between devices: 0.37 us -> 22.6 us
    reduce_scatter x4 -> x1, waiting for transfers between devices: 443 us -> 71.2 us  [per_device(): lax.psum_scatter(ffn_grads, ('head', 'row'), scatter_dimension=0, tiled=T...]
    dot_general x48 -> x0, matrix products: 235 us -> none  [the longest x12 50 us: scores_of(): jnp.einsum('ihe,jhe->hij', query_row, key_row, preferred_element_type=jnp...]
    pallas_call x0 -> x5, Pallas kernels: none -> 183 us  [the longest x1 49.2 us: attend(): pl.pallas_call(body, grid_spec=pltpu.PrefetchScalarGridSpec(num_scalar_pr...]
    all_gather x4 -> x1, waiting for transfers between devices: 136 us -> 0.02 us  [per_device(): lax.all_gather(jnp.stack([w_in.T, w_down])[None], ('head', 'row'), axis=0...]
    ppermute x0 -> x18, waiting for transfers between devices: none -> 112 us  [swap(): return lax.ppermute(value, 'head', [(i, i ^ k) for i in range(nh)])]
    dynamic_update_slice x24 -> x0, local copies, waits for them, and re-layouts: 87.1 us -> none  [per_device(): lax.map(attend_row, (queries, key_rows, value_rows, prev_logits, segment_...]
    psum x2, blocking collectives: 56.9 us -> 139 us  [the longest x1 123 us: per_device(): lax.psum((jnp.concatenate([sums_two[:3], sums_one[:3]]), gb_in.reshape(-1...]
    dynamic_slice x24 -> x1, local copies, waits for them, and re-layouts: 51.7 us -> 0.59 us  [per_device(): grad_b_in = lax.dynamic_slice_in_dim(grad_b_in, place * shard, shard)]
  transfers between devices with their start and end apart: 9 -> 21, of which waited for: 6 -> 7; matrix products, arithmetic and copies ran while one was open for 9% -> 5% of each run, Pallas kernels for 0% -> 18%
where the time goes in v1:
time: 631 us; the launch traced here: 630 us
  waiting for transfers between devices  184 us (29%)
  Pallas kernels  183 us (29%)
  blocking collectives  182 us (29%)
  local copies, waits for them, and re-layouts  28 us (4%)
  starting transfers between devices  22.6 us (4%)
  other arithmetic  17.5 us (3%)
  between operations  14.1 us (2%)
    psum x1, blocking collectives, per_device(): lax.psum((jnp.concatenate([sums_two[:3], sums_one[:3]]), gb_in.reshape(-1...  123 us
    ppermute x18, waiting for transfers between devices, swap(): return lax.ppermute(value, 'head', [(i, i ^ k) for i in range(nh)])  112 us
    reduce_scatter x1, waiting for transfers between devices, per_device(): lax.psum_scatter(ffn_grads, ('head', 'row'), scatter_dimension=0, tiled=T...  71.2 us
    pallas_call x1, Pallas kernels, attend(): pl.pallas_call(body, grid_spec=pltpu.PrefetchScalarGridSpec(num_scalar_pr...  49.2 us
    pallas_call x1, Pallas kernels, attend_back(): pl.pallas_call(body, grid_spec=pltpu.PrefetchScalarGridSpec(num_scalar_pr...  45.7 us
    all_gather x1, blocking collectives, per_device(): lax.all_gather(b_in.astype(f32), ('head', 'row'), axis=0, tiled=True)  42.6 us
    pallas_call x1, Pallas kernels, feed_forward(): pl.pallas_call(body, grid=(blocks,), in_specs=[whole((count, cols))] * nh...  35.9 us
    pallas_call x1, Pallas kernels, feed_back(): pl.pallas_call(body, grid=(blocks,), in_specs=[whole((count, cols))] * nh...  32.2 us
  transfers between devices with their start and end apart: 21, of which 7 were waited for; matrix products, arithmetic and copies ran while one was open for 5% of the time, Pallas kernels for 18%

profile of v1, /device:TPU:0, one launch (start us, length us, event | category | flops | bytes accessed | tf_op | source)
XLA Modules:
  0.0 630.4 jit_solution(13681003113890268644)
XLA Ops:
  10.3 4.0 collective-permute-start.2
  14.9 2.8 collective-permute-start.8
  21.2 2.6 copy.45
  23.8 2.7 copy.46.refs_4_.refs_14_
  26.5 26.8 %collective-permute-done.2.refs_3_ = bf16[6,128,1024]{2,1,0:T(8,128)(2,1)S(1)} collective-permute-done((bf16[6,128,1024]{2,1,0:T(8,128)(2,1)S(1)}, bf16[6,128,1024]{2,1,0:T(8,128)(2,1)S(1)}, u32[]{:S(2)}, u32[]{:S(2)}) %collective-permute-start.2) | collective-permute-done | bytes 1572896 | tf_op jit(solution)/shard_map/ppermute | solution.py:528
  55.3 38.5 %collective-permute-done.1.refs_2_ = bf16[6,128,1024]{2,1,0:T(8,128)(2,1)} collective-permute-done((bf16[6,128,1024]{2,1,0:T(8,128)(2,1)S(1)}, bf16[6,128,1024]{2,1,0:T(8,128)(2,1)}, u32[]{:S(2)}, u32[]{:S(2)}) %collective-permute-start.1) | collective-permute-done | bytes 1572896 | tf_op jit(solution)/shard_map/ppermute | solution.py:528
  93.9 8.3 %collective-permute-done.refs_1_ = bf16[6,128,1024]{2,1,0:T(8,128)(2,1)} collective-permute-done((bf16[6,128,1024]{2,1,0:T(8,128)(2,1)S(1)}, bf16[6,128,1024]{2,1,0:T(8,128)(2,1)}, u32[]{:S(2)}, u32[]{:S(2)}) %collective-permute-start) | collective-permute-done | bytes 1572896 | tf_op jit(solution)/shard_map/ppermute | solution.py:528
  102.1 49.2 %attend.1 = (bf16[6,512,768]{2,1,0:T(8,128)(2,1)}, bf16[6,4,512,512]{3,2,1,0:T(8,128)(2,1)}, bf16[4,6,128,256]{3,2,1,0:T(8,128)(2,1)}, f32[6,512,128]{2,1,0:T(8,128)}) custom-call(s32[1]{0:T(128)} %bitcast.me_ref, bf16[6,128,1024]{2,1,0:T(8,128)(2,1)} %refs_0_.3, bf16[6,128,1024]{2,1,0:T(8,128)(2,1)} %collective-permute-done.refs_1_, ...), custom_call_target="tpu_custom_call" | custom-call | tf_op jit(solution)/shard_map/attend/pallas_call | solution.py:114
  153.6 3.4 collective-permute-start.5
  157.9 42.6 %all-gather.1 = f32[32,1,128]{2,1,0:T(1,128)} all-gather(f32[1,1,128]{2,1,0:T(1,128)S(1)} %bitcast_convert_fusion), channel_id=1, replica_groups=mesh['head'=4,'row'=8] {'head','row'}, dimensions={0}, use_global_device_ids=true | all-gather | bytes 16896 | tf_op jit(solution)/shard_map/all_gather | solution.py:533
  201.5 35.9 %feed_forward.1 = (bf16[768,1024]{1,0:T(8,128)(2,1)}, bf16[768,1024]{1,0:T(8,128)(2,1)}, f32[768,1024]{1,0:T(8,128)}, f32[768,128]{1,0:T(8,128)}, f32[768,1024]{...) custom-call(bf16[768,256]{1,0:T(8,128)(2,1)} %bitcast.77, ...), custom_call_target="tpu_custom_call" | custom-call | tf_op jit(solution)/shard_map/feed_forward/pallas_call | solution.py:345
  237.4 32.2 %feed_back.1 = (f32[768,1024]{1,0:T(8,128)}, bf16[4,768,256]{2,1,0:T(8,128)(2,1)}, bf16[4,256,1024]{2,1,0:T(8,128)(2,1)}, bf16[768,4096]{1,0:T(8,128)(2,1)}, f32[8,1,512]{2,1,0:T(1,128)}, /*index=5*/f32[8,1024]{1,0:T(8,128)}) custom-call(bf16[768,256]{1,0:T(8,128)(2,1)} %bitcast.78, bf16[768,256]{1,0:T(8,128)(2,1)} %copy-done.6, bf16[768,256]{1,0:T(8,128)(2,1)} %copy-done.4, ...), custom_call_target="tpu_custom_call" | custom-call | tf_op jit(solution)/shard_map/feed_back/pallas_call | solution.py:435
  269.6 2.3 fusion.7
  278.7 5.2 collective-permute-done.10.refs_6_
  283.9 25.4 %collective-permute-done.11.refs_7_ = bf16[6,128,256]{2,1,0:T(8,128)(2,1)S(1)} collective-permute-done((bf16[6,128,256]{2,1,0:T(8,128)(2,1)S(1)}, bf16[6,128,256]{2,1,0:T(8,128)(2,1)S(1)}, u32[]{:S(2)}, u32[]{:S(2)}) %collective-permute-start.11) | collective-permute-done | bytes 393248 | tf_op jit(solution)/shard_map/ppermute | solution.py:528
  309.3 8.1 %collective-permute-done.9.refs_5_ = bf16[6,128,256]{2,1,0:T(8,128)(2,1)S(1)} collective-permute-done((bf16[6,128,256]{2,1,0:T(8,128)(2,1)S(1)}, bf16[6,128,256]{2,1,0:T(8,128)(2,1)S(1)}, u32[]{:S(2)}, u32[]{:S(2)}) %collective-permute-start.9) | collective-permute-done | bytes 393248 | tf_op jit(solution)/shard_map/ppermute | solution.py:528
  318.1 45.7 %attend_back.1 = (bf16[6,4,512,512]{3,2,1,0:T(8,128)(2,1)}, bf16[4,6,128,1024]{3,2,1,0:T(8,128)(2,1)}, f32[768,1024]{1,0:T(8,128)}, f32[8,768]{1,0:T(8,128)}) custom-call(s32[1]{0:T(128)} %bitcast.me_ref, bf16[6,128,1024]{2,1,0:T(8,128)(2,1)} %refs_0_.3, bf16[6,128,1024]{2,1,0:T(8,128)(2,1)} %collective-permute-done.refs_1_, ...), custom_call_target="tpu_custom_call" | custom-call | tf_op jit(solution)/shard_map/attend_back/pallas_call | solution.py:214
  369.8 19.7 %weight_grads.1 = bf16[32,2,128,1024]{3,2,1,0:T(8,128)(2,1)} custom-call(bf16[768,1024]{1,0:T(8,128)(2,1)} %get-tuple-element.58.x_ref, bf16[768,1024]{1,0:T(8,128)(2,1)} %get-tuple-element.43.refs_9_.gf_ref, bf16[768,4096]{1,0:T(8,128)(2,1)} %get-tuple-element.59.gh_ref, bf16[768,4096]{1,0:T(8,128)(2,1)} %get-tuple-element.60.act_ref), custom_call_target="tpu_custom_call" | custom-call | tf_op jit(solution)/shard_map/weight_grads/pallas_call | solution.py:483
  389.5 4.8 slice_bitcast_fusion.2
  397.9 122.9 %all-reduce = (f32[6,1024]{1,0:T(8,128)S(1)}, f32[4096]{0:T(1024)S(1)}) all-reduce(f32[6,1024]{1,0:T(8,128)S(1)} %pad_maximum_fusion.1, f32[4096]{0:T(1024)S(1)} %bitcast.92), channel_id=1, replica_groups=mesh['head'=4,'row'=8] {'head','row'}, use_global_device_ids=true, to_apply=%region_3.0 | all-reduce | flops 10240 | bytes 81920 | tf_op jit(solution)/shard_map/psum | solution.py:582
  522.8 16.4 %psum.36 = f32[2,256]{1,0:T(2,128)} all-reduce(f32[2,256]{1,0:T(2,128)S(1)} %pad_maximum_fusion.3), channel_id=1, replica_groups=mesh['head'=4,'row'=8] {'row'}, use_global_device_ids=true, to_apply=%region_1.0 | all-reduce | flops 512 | bytes 4096 | tf_op jit(solution)/shard_map/psum | solution.py:581
  539.2 2.3 convert_element_type.76
  544.5 5.2 fusion.2
  549.7 71.2 %reduce-scatter.2.cloned.1.call-done = bf16[1,2,128,1024]{3,2,1,0:T(8,128)(2,1)} async-done(((bf16[32,2,128,1024]{3,2,1,0:T(8,128)(2,1)}), bf16[1,2,128,1024]{3,2,1,0:T(8,128)(2,1)}) %reduce-scatter.2.cloned.1.call-update) | async-done | bytes 524304 | tf_op jit(solution)/shard_map/reduce_scatter | solution.py:567
  (109 shorter events, 38.0 us)
Async XLA Ops:
  7.2 11.7 %copy-start.11 = (s32[6,512]{1,0:T(8,128)S(1)}, s32[6,512]{1,0:T(8,128)}, u32[]{:S(2)}) copy-start(s32[6,512]{1,0:T(8,128)} %param.19) | copy-start | bytes 36868
  7.2 193.3 %all-gather.4.cloned.1.call-start = ((), (), s32[]{:S(2)}) async-start(), calls=%async_computation.2 | async-start | bytes 17301504 | tf_op jit(solution)/shard_map/all_gather | solution.py:532
  10.3 528.9 %all-reduce.4.cloned.1.call-start = ((), (), s32[]{:S(2)}) async-start(), calls=%async_computation.3 | async-start | bytes 4194304 | tf_op jit(solution)/shard_map/psum | solution.py:579
  10.3 43.0 %collective-permute-start.2 = (bf16[6,128,1024]{2,1,0:T(8,128)(2,1)S(1)}, bf16[6,128,1024]{2,1,0:T(8,128)(2,1)S(1)}, u32[]{:S(2)}, u32[]{:S(2)}) collective-permute-start(bf16[6,128,1024]{2,1,0:T(8,128)(2,1)S(1)} %copy-done), channel_id=1, source_target_pairs={{0,24},{8,16},{16,8},{24,0},{1,25},{9,17},{17,9},{25,1},{2,26},{10... | collective-permute-start | bytes 4718600 | tf_op jit(solution)/shard_map/ppermute | solution.py:528
  14.3 79.6 %collective-permute-start.1 = (bf16[6,128,1024]{2,1,0:T(8,128)(2,1)S(1)}, bf16[6,128,1024]{2,1,0:T(8,128)(2,1)}, u32[]{:S(2)}, u32[]{:S(2)}) collective-permute-start(bf16[6,128,1024]{2,1,0:T(8,128)(2,1)S(1)} %copy-done), channel_id=1, source_target_pairs={{0,16},{8,24},{16,0},{24,8},{1,17},{9,25},{17,1},{25,9},{2,18},{10... | collective-permute-start | bytes 4718600 | tf_op jit(solution)/shard_map/ppermute | solution.py:528
  14.8 87.3 %collective-permute-start = (bf16[6,128,1024]{2,1,0:T(8,128)(2,1)S(1)}, bf16[6,128,1024]{2,1,0:T(8,128)(2,1)}, u32[]{:S(2)}, u32[]{:S(2)}) collective-permute-start(bf16[6,128,1024]{2,1,0:T(8,128)(2,1)S(1)} %copy-done), channel_id=1, source_target_pairs={{0,8},{8,0},{16,24},{24,16},{1,9},{9,1},{17,25},{25,17},{2,10},{10... | collective-permute-start | bytes 4718600 | tf_op jit(solution)/shard_map/ppermute | solution.py:528
  14.9 142.1 %collective-permute-start.8 = (bf16[256,1024]{1,0:T(8,128)(2,1)}, bf16[256,1024]{1,0:T(8,128)(2,1)}, u32[]{:S(2)}, u32[]{:S(2)}) collective-permute-start(bf16[256,1024]{1,0:T(8,128)(2,1)} %refs_4_.3), channel_id=1, source_target_pairs={{0,24},{8,16},{16,8},{24,0},{1,25},{9,17},{17,9},{25,1},{2,26},{10... | collective-permute-start | bytes 1572872 | tf_op jit(solution)/shard_map/ppermute | solution.py:528
  17.8 182.7 %collective-permute-start.7 = (bf16[256,1024]{1,0:T(8,128)(2,1)}, bf16[256,1024]{1,0:T(8,128)(2,1)}, u32[]{:S(2)}, u32[]{:S(2)}) collective-permute-start(bf16[256,1024]{1,0:T(8,128)(2,1)} %refs_4_.3), channel_id=1, source_target_pairs={{0,16},{8,24},{16,0},{24,8},{1,17},{9,25},{17,1},{25,9},{2,18},{10... | collective-permute-start | bytes 1572872 | tf_op jit(solution)/shard_map/ppermute | solution.py:528
  53.3 48.8 %copy-start.1 = (bf16[6,128,1024]{2,1,0:T(8,128)(2,1)}, bf16[6,128,1024]{2,1,0:T(8,128)(2,1)S(1)}, u32[]{:S(2)}) copy-start(bf16[6,128,1024]{2,1,0:T(8,128)(2,1)S(1)} %collective-permute-done.2.refs_3_) | copy-start | bytes 4718596
  53.3 147.1 %collective-permute-start.6 = (bf16[256,1024]{1,0:T(8,128)(2,1)}, bf16[256,1024]{1,0:T(8,128)(2,1)}, u32[]{:S(2)}, u32[]{:S(2)}) collective-permute-start(bf16[256,1024]{1,0:T(8,128)(2,1)} %refs_4_.3), channel_id=1, source_target_pairs={{0,8},{8,0},{16,24},{24,16},{1,9},{9,1},{17,25},{25,17},{2,10},{10... | collective-permute-start | bytes 1572872 | tf_op jit(solution)/shard_map/ppermute | solution.py:528
  153.6 46.8 %collective-permute-start.4 = (bf16[768,256]{1,0:T(8,128)(2,1)S(1)}, bf16[768,256]{1,0:T(8,128)(2,1)S(1)}, u32[]{:S(2)}, u32[]{:S(2)}) collective-permute-start(bf16[768,256]{1,0:T(8,128)(2,1)S(1)} %bitcast.86), channel_id=1, source_target_pairs={{0,16},{8,24},{16,0},{24,8},{1,17},{9,25},{17,1},{25,9},{2,18},{10... | collective-permute-start | bytes 1179656 | tf_op jit(solution)/shard_map/ppermute | solution.py:528
  153.6 46.8 %collective-permute-start.5 = (bf16[768,256]{1,0:T(8,128)(2,1)S(1)}, bf16[768,256]{1,0:T(8,128)(2,1)S(1)}, u32[]{:S(2)}, u32[]{:S(2)}) collective-permute-start(bf16[768,256]{1,0:T(8,128)(2,1)S(1)} %bitcast.84), channel_id=1, source_target_pairs={{0,24},{8,16},{16,8},{24,0},{1,25},{9,17},{17,9},{25,1},{2,26},{10... | collective-permute-start | bytes 1179656 | tf_op jit(solution)/shard_map/ppermute | solution.py:528
  157.0 43.5 %collective-permute-start.3 = (bf16[768,256]{1,0:T(8,128)(2,1)S(1)}, bf16[768,256]{1,0:T(8,128)(2,1)S(1)}, u32[]{:S(2)}, u32[]{:S(2)}) collective-permute-start(bf16[768,256]{1,0:T(8,128)(2,1)S(1)} %bitcast.83), channel_id=1, source_target_pairs={{0,8},{8,0},{16,24},{24,16},{1,9},{9,1},{17,25},{25,17},{2,10},{10... | collective-permute-start | bytes 1179656 | tf_op jit(solution)/shard_map/ppermute | solution.py:528
  271.9 11.9 %collective-permute-start.10 = (bf16[6,128,256]{2,1,0:T(8,128)(2,1)S(1)}, bf16[6,128,256]{2,1,0:T(8,128)(2,1)S(1)}, u32[]{:S(2)}, u32[]{:S(2)}) collective-permute-start(bf16[6,128,256]{2,1,0:T(8,128)(2,1)S(1)} %bitcast.88), channel_id=1, source_target_pairs={{0,16},{8,24},{16,0},{24,8},{1,17},{9,25},{17,1},{25,9},{2,18},{10... | collective-permute-start | bytes 1179656 | tf_op jit(solution)/shard_map/ppermute | solution.py:528
  275.2 92.3 %collective-permute-start.15 = (bf16[256,1024]{1,0:T(8,128)(2,1)}, bf16[256,1024]{1,0:T(8,128)(2,1)S(1)}, u32[]{:S(2)}, u32[]{:S(2)}) collective-permute-start(bf16[256,1024]{1,0:T(8,128)(2,1)} %get-tuple-element.117), channel_id=1, source_target_pairs={{0,8},{8,0},{16,24},{24,16},{1,9},{9,1},{17,25},{25,17},{2,10},{10... | collective-permute-start | bytes 1572872 | tf_op jit(solution)/shard_map/ppermute | solution.py:528
  275.2 92.3 %collective-permute-start.17 = (bf16[256,1024]{1,0:T(8,128)(2,1)}, bf16[256,1024]{1,0:T(8,128)(2,1)S(1)}, u32[]{:S(2)}, u32[]{:S(2)}) collective-permute-start(bf16[256,1024]{1,0:T(8,128)(2,1)} %get-tuple-element.118), channel_id=1, source_target_pairs={{0,24},{8,16},{16,8},{24,0},{1,25},{9,17},{17,9},{25,1},{2,26},{10... | collective-permute-start | bytes 1572872 | tf_op jit(solution)/shard_map/ppermute | solution.py:528
  276.6 90.9 %collective-permute-start.16 = (bf16[256,1024]{1,0:T(8,128)(2,1)}, bf16[256,1024]{1,0:T(8,128)(2,1)S(1)}, u32[]{:S(2)}, u32[]{:S(2)}) collective-permute-start(bf16[256,1024]{1,0:T(8,128)(2,1)} %get-tuple-element.119), channel_id=1, source_target_pairs={{0,16},{8,24},{16,0},{24,8},{1,17},{9,25},{17,1},{25,9},{2,18},{10... | collective-permute-start | bytes 1572872 | tf_op jit(solution)/shard_map/ppermute | solution.py:528
  278.7 30.6 %collective-permute-start.11 = (bf16[6,128,256]{2,1,0:T(8,128)(2,1)S(1)}, bf16[6,128,256]{2,1,0:T(8,128)(2,1)S(1)}, u32[]{:S(2)}, u32[]{:S(2)}) collective-permute-start(bf16[6,128,256]{2,1,0:T(8,128)(2,1)S(1)} %bitcast.87), channel_id=1, source_target_pairs={{0,24},{8,16},{16,8},{24,0},{1,25},{9,17},{17,9},{25,1},{2,26},{10... | collective-permute-start | bytes 1179656 | tf_op jit(solution)/shard_map/ppermute | solution.py:528
  283.9 33.5 %copy-start.8 = (bf16[6,128,256]{2,1,0:T(8,128)(2,1)}, bf16[6,128,256]{2,1,0:T(8,128)(2,1)S(1)}, u32[]{:S(2)}) copy-start(bf16[6,128,256]{2,1,0:T(8,128)(2,1)S(1)} %collective-permute-done.10.refs_6_) | copy-start | bytes 1179652
  283.9 33.5 %collective-permute-start.9 = (bf16[6,128,256]{2,1,0:T(8,128)(2,1)S(1)}, bf16[6,128,256]{2,1,0:T(8,128)(2,1)S(1)}, u32[]{:S(2)}, u32[]{:S(2)}) collective-permute-start(bf16[6,128,256]{2,1,0:T(8,128)(2,1)S(1)} %bitcast.85), channel_id=1, source_target_pairs={{0,8},{8,0},{16,24},{24,16},{1,9},{9,1},{17,25},{25,17},{2,10},{10... | collective-permute-start | bytes 1179656 | tf_op jit(solution)/shard_map/ppermute | solution.py:528
  369.7 251.2 %reduce-scatter.2.cloned.1.call-start = ((), (), s32[]{:S(2)}) async-start(), calls=%async_computation.1 | async-start | bytes 17301504 | tf_op jit(solution)/shard_map/reduce_scatter | solution.py:567
  394.3 149.0 %collective-permute-start.12 = (bf16[6,128,1024]{2,1,0:T(8,128)(2,1)}, bf16[6,128,1024]{2,1,0:T(8,128)(2,1)S(1)}, u32[]{:S(2)}, u32[]{:S(2)}) collective-permute-start(bf16[6,128,1024]{2,1,0:T(8,128)(2,1)} %get-tuple-element.114), channel_id=1, source_target_pairs={{0,8},{8,0},{16,24},{24,16},{1,9},{9,1},{17,25},{25,17},{2,10},{10... | collective-permute-start | bytes 4718600 | tf_op jit(solution)/shard_map/ppermute | solution.py:528
  394.4 148.9 %collective-permute-start.14 = (bf16[6,128,1024]{2,1,0:T(8,128)(2,1)}, bf16[6,128,1024]{2,1,0:T(8,128)(2,1)S(1)}, u32[]{:S(2)}, u32[]{:S(2)}) collective-permute-start(bf16[6,128,1024]{2,1,0:T(8,128)(2,1)} %get-tuple-element.115), channel_id=1, source_target_pairs={{0,24},{8,16},{16,8},{24,0},{1,25},{9,17},{17,9},{25,1},{2,26},{10... | collective-permute-start | bytes 4718600 | tf_op jit(solution)/shard_map/ppermute | solution.py:528
  395.9 147.5 %collective-permute-start.13 = (bf16[6,128,1024]{2,1,0:T(8,128)(2,1)}, bf16[6,128,1024]{2,1,0:T(8,128)(2,1)}, u32[]{:S(2)}, u32[]{:S(2)}) collective-permute-start(bf16[6,128,1024]{2,1,0:T(8,128)(2,1)} %get-tuple-element.116), channel_id=1, source_target_pairs={{0,16},{8,24},{16,0},{24,8},{1,17},{9,25},{17,1},{25,9},{2,18},{10... | collective-permute-start | bytes 4718600 | tf_op jit(solution)/shard_map/ppermute | solution.py:528
  (20 other events, 102.0 us)
Sparse Core Ops, SparseCore 0:
  11.6 164.4 all-gather.3
  369.8 61.4 all-reduce.3
  433.6 187.2 reduce-scatter.1
